TPU v7x, 256 devices: a whole 4x4x8 slice. The times are simulated.
256 devices in a mesh: ctx: 32 (over y, x, core), fsdp: 4 (over z_hi), tp: 2 (over z_lo).
Axes of the slice: x: 4, y: 4, z: 8 (z_hi: 4, z_lo: 2; z = z_hi * 2 + z_lo), core: 2. Of those that a mesh axis runs over, the one named last changes fastest.
Arguments:
- query_gate: bfloat16 [4, 4096, 8192], P('fsdp', 'ctx', 'tp'), may hold values from -6 to 6
- key_proj: bfloat16 [4, 4096, 8192], P('fsdp', 'ctx', 'tp'), may hold values from -6 to 6
- value_proj: bfloat16 [4, 4096, 8192], P('fsdp', 'ctx', 'tp'), may hold values from -6 to 6
- grad_out: bfloat16 [4, 4096, 8192], P('fsdp', 'ctx', 'tp'), may hold values from -6 to 6
- filters: float32 [128, 8192], P('fsdp', 'tp'), may hold values from -0.5 to 0.5
- doc_bounds: int32 [4, 49], P('fsdp'), may hold values from 0 to 4032, as said below
- continues: int32 [4, 32], P('fsdp', 'ctx'), may hold values from 0 to 1, as said below
Outputs:
- grad_query: bfloat16 [4, 4096, 8192], P('fsdp', 'ctx', 'tp')
- grad_key: bfloat16 [4, 4096, 8192], P('fsdp', 'ctx', 'tp')
- grad_value: bfloat16 [4, 4096, 8192], P('fsdp', 'ctx', 'tp')
- grad_filter: float32 [128, 8192], P('fsdp', 'tp')
Inputs may be any that keep to these rules, and one draw needn't show every extreme that they name: Each row of doc_bounds increases strictly and begins with 0. continues[w, d] is 0 for d = 0 and wherever a document of window w begins at token d * 128; at other shard edges it may be 0 or 1 (the sequence is cut there or not).
All inputs are finite; a program needn't handle non-finite values.
Results may differ from a plain program's by a relative error of at most 0.0065.
Values may be sent and summed in bfloat16 or wider, within the bound.
A program may use at most 64 MiB of HBM per device.

v0:
```python
import math
import jax
import jax.numpy as jnp
from jax import lax
from jax.sharding import PartitionSpec as P

tap_group = 16


def from_behind(array, axis, by):
    count = lax.axis_size(axis)
    pairs = [(i, i + by) for i in range(count) if 0 <= i + by < count]
    return lax.ppermute(array, axis, pairs)


def doc_starts(bound_row, positions):
    below = bound_row[None, :] <= positions[:, None]
    return jnp.max(jnp.where(below, bound_row[None, :], 0), axis=1)


def shards(query_gate, key_proj, value_proj, grad_out, filters, doc_bounds, continues):
    weights = lax.all_gather(filters, "fsdp", axis=0, tiled=True)
    filter_len = weights.shape[0]
    length = query_gate.shape[1]
    shard_index = lax.axis_index("ctx")
    first_token = shard_index * length
    positions = first_token + jnp.arange(length, dtype=jnp.int32)
    bound_row = doc_bounds[0]
    own_flag = continues[0, 0]
    plain_starts = doc_starts(bound_row, positions)
    own_starts = jnp.where(own_flag == 1, plain_starts, jnp.maximum(plain_starts, first_token))
    later_positions = first_token + length + jnp.arange(filter_len, dtype=jnp.int32)
    reach_starts = jnp.concatenate([own_starts, doc_starts(bound_row, later_positions)])
    query_local = query_gate[0]
    key_local = key_proj[0]
    value_local = value_proj[0]
    grad_local = grad_out[0]
    channels = query_local.shape[1]
    mixed_input = (key_local.astype(jnp.float32) * value_local.astype(jnp.float32)).astype(
        jnp.bfloat16
    )
    rows_before = from_behind(mixed_input, "ctx", 1)
    mixed_ext = jnp.concatenate([rows_before, mixed_input], axis=0)
    grad_conv = (grad_local.astype(jnp.float32) * query_local.astype(jnp.float32)).astype(
        jnp.bfloat16
    )
    send_rows = jnp.where(own_flag == 1, grad_conv, jnp.zeros_like(grad_conv))
    rows_after = from_behind(send_rows, "ctx", -1)
    grad_ext = jnp.concatenate([grad_conv, rows_after], axis=0)
    grad_wide = grad_conv.astype(jnp.float32)

    def tap_block(group_index, state_tuple):
        conv_out, grad_back, filt_grad = state_tuple
        for offset in range(tap_group):
            tap_index = group_index * tap_group + offset
            weight_row = lax.dynamic_slice_in_dim(weights, tap_index, 1, 0)
            earlier = lax.dynamic_slice_in_dim(mixed_ext, filter_len - tap_index, length, 0).astype(
                jnp.float32
            )
            inside = (positions - tap_index >= own_starts)[:, None]
            conv_out = conv_out + jnp.where(inside, earlier * weight_row, 0.0)
            tap_term = jnp.sum(jnp.where(inside, grad_wide * earlier, 0.0), axis=0)
            filt_grad = lax.dynamic_update_slice_in_dim(filt_grad, tap_term[None, :], tap_index, 0)
            ahead_rows = lax.dynamic_slice_in_dim(grad_ext, tap_index, length, 0).astype(
                jnp.float32
            )
            reaching = (positions >= lax.dynamic_slice_in_dim(reach_starts, tap_index, length, 0))[
                :, None
            ]
            grad_back = grad_back + jnp.where(reaching, ahead_rows * weight_row, 0.0)
        return (conv_out, grad_back, filt_grad)

    start_state = (
        jnp.zeros((length, channels), jnp.float32),
        jnp.zeros((length, channels), jnp.float32),
        jnp.zeros((filter_len, channels), jnp.float32),
    )
    conv_out, grad_back, filt_grad = lax.fori_loop(
        jnp.int32(0), jnp.int32(filter_len // tap_group), tap_block, start_state
    )
    grad_query = (grad_local.astype(jnp.float32) * conv_out).astype(jnp.bfloat16)
    grad_key = (grad_back * value_local.astype(jnp.float32)).astype(jnp.bfloat16)
    grad_value = (grad_back * key_local.astype(jnp.float32)).astype(jnp.bfloat16)
    norm_scale = 1.0 / math.sqrt(lax.axis_size("fsdp") * lax.axis_size("ctx") * length)
    filt_grad = filt_grad * norm_scale
    summed_all = lax.psum(filt_grad, "ctx")
    share_out = lax.psum_scatter(summed_all, "fsdp", scatter_dimension=0, tiled=True)
    return (grad_query[None], grad_key[None], grad_value[None], share_out)


def solution(mesh):
    in_specs = (
        P("fsdp", "ctx", "tp"),
        P("fsdp", "ctx", "tp"),
        P("fsdp", "ctx", "tp"),
        P("fsdp", "ctx", "tp"),
        P("fsdp", "tp"),
        P("fsdp", None),
        P("fsdp", "ctx"),
    )
    out_specs = (
        P("fsdp", "ctx", "tp"),
        P("fsdp", "ctx", "tp"),
        P("fsdp", "ctx", "tp"),
        P("fsdp", "tp"),
    )
    return jax.shard_map(shards, mesh=mesh, in_specs=in_specs, out_specs=out_specs, check_vma=False)
```

profile of v0, /device:TPU:1, one launch (start us, length us, event | category | flops | bytes accessed | tf_op | source)
XLA Modules:
  0.0 783.8 jit_solution(15440662783563626389)
XLA Ops:
  20.8 5.3 collective-permute-done
  28.0 6.5 collective-permute-done.1
  37.2 25.2 %all-gather.2.cloned.1.call-done = f32[128,4096]{1,0:T(8,128)} async-done(((f32[32,4096]{1,0:T(8,128)}), f32[128,4096]{1,0:T(8,128)}) %all-gather.2.cloned.1.call-update) | async-done | bytes 2097168 | tf_op jit(solution)/shard_map/all_gather | solution.py:22
  63.9 540.4 %while.18 = (s32[]{:T(128)}, f32[128,4096]{1,0:T(8,128)}, f32[128,4096]{1,0:T(8,128)}, f32[128,4096]{1,0:T(8,128)}, s32[128]{0:T(128)S(1)}, /*index=5*/bf16[256,...) while((s32[]{:T(128)}, f32[128,4096]{1,0:T(8,128)}, ...), condition=%wide.region_19.20_spmd.clone, body=%wide.region_2.19_spmd.clone.sunk | while | flops 101652864 | bytes 89937200 | solution.py:78
  64.1 6.7 fusion.150
  70.8 5.3 fusion.149
  104.1 15.4 %fusion.148 = f32[128,4096]{1,0:T(8,128)} fusion(f32[128,4096]{1,0:T(8,128)} %get-tuple-element.669, bf16[256,4096]{1,0:T(8,128)(2,1)} %get-tuple-element.736, s32[]{:T(128)S(6)} %select_n.1126, s32[]{:T(128)S(6)} %select_n.1127, s32[]{:T(128)S(6)} %select_n.1128, s32[]{:T(128)S(6)} %select_n.1129, s32[]{:T(128)S(6)} %select_n.1130, ...), kind=kLoop, calls=%fused_computation.112.clone.1 | loop fusion | flops 34078720 | bytes 21235776 | tf_op jit(solution)/shard_map/while/body/add | solution.py:70
  119.5 10.1 %fusion.146 = f32[128,4096]{1,0:T(8,128)S(1)} fusion(f32[128,4096]{1,0:T(8,128)S(1)} %copy-done.2, f32[4096]{0:T(1024)S(1)} %bitcast.124, f32[4096]{0:T(1024)S(1)} %bitcast.126, f32[4096]{0:T(1024)S(1)} %bitcast.128, f32[4096]{0:T(1024)S(1)} %bitcast.130, f32[4096]{0:T(1024)S(1)} %bitcast.132, f32[4096]{0:T(1024)S(1)} %bitcast.134, ...), kind=kLoop, calls=%fused_computation.49.clone.1 | loop fusion | flops 34078720 | bytes 21235776 | tf_op jit(solution)/shard_map/while/body/add | solution.py:61
  131.2 6.7 fusion.150
  137.9 5.3 fusion.149
  171.3 15.7 %fusion.148 = f32[128,4096]{1,0:T(8,128)} fusion(f32[128,4096]{1,0:T(8,128)} %get-tuple-element.669, bf16[256,4096]{1,0:T(8,128)(2,1)} %get-tuple-element.736, s32[]{:T(128)S(6)} %select_n.1126, s32[]{:T(128)S(6)} %select_n.1127, s32[]{:T(128)S(6)} %select_n.1128, s32[]{:T(128)S(6)} %select_n.1129, s32[]{:T(128)S(6)} %select_n.1130, ...), kind=kLoop, calls=%fused_computation.112.clone.1 | loop fusion | flops 34078720 | bytes 21235776 | tf_op jit(solution)/shard_map/while/body/add | solution.py:70
  187.1 10.1 %fusion.146 = f32[128,4096]{1,0:T(8,128)S(1)} fusion(f32[128,4096]{1,0:T(8,128)S(1)} %copy-done.2, f32[4096]{0:T(1024)S(1)} %bitcast.124, f32[4096]{0:T(1024)S(1)} %bitcast.126, f32[4096]{0:T(1024)S(1)} %bitcast.128, f32[4096]{0:T(1024)S(1)} %bitcast.130, f32[4096]{0:T(1024)S(1)} %bitcast.132, f32[4096]{0:T(1024)S(1)} %bitcast.134, ...), kind=kLoop, calls=%fused_computation.49.clone.1 | loop fusion | flops 34078720 | bytes 21235776 | tf_op jit(solution)/shard_map/while/body/add | solution.py:61
  198.7 6.7 fusion.150
  238.9 15.9 %fusion.148 = f32[128,4096]{1,0:T(8,128)} fusion(f32[128,4096]{1,0:T(8,128)} %get-tuple-element.669, bf16[256,4096]{1,0:T(8,128)(2,1)} %get-tuple-element.736, s32[]{:T(128)S(6)} %select_n.1126, s32[]{:T(128)S(6)} %select_n.1127, s32[]{:T(128)S(6)} %select_n.1128, s32[]{:T(128)S(6)} %select_n.1129, s32[]{:T(128)S(6)} %select_n.1130, ...), kind=kLoop, calls=%fused_computation.112.clone.1 | loop fusion | flops 34078720 | bytes 21235776 | tf_op jit(solution)/shard_map/while/body/add | solution.py:70
  254.9 10.1 %fusion.146 = f32[128,4096]{1,0:T(8,128)S(1)} fusion(f32[128,4096]{1,0:T(8,128)S(1)} %copy-done.2, f32[4096]{0:T(1024)S(1)} %bitcast.124, f32[4096]{0:T(1024)S(1)} %bitcast.126, f32[4096]{0:T(1024)S(1)} %bitcast.128, f32[4096]{0:T(1024)S(1)} %bitcast.130, f32[4096]{0:T(1024)S(1)} %bitcast.132, f32[4096]{0:T(1024)S(1)} %bitcast.134, ...), kind=kLoop, calls=%fused_computation.49.clone.1 | loop fusion | flops 34078720 | bytes 21235776 | tf_op jit(solution)/shard_map/while/body/add | solution.py:61
  266.5 6.7 fusion.150
  306.4 16.0 %fusion.148 = f32[128,4096]{1,0:T(8,128)} fusion(f32[128,4096]{1,0:T(8,128)} %get-tuple-element.669, bf16[256,4096]{1,0:T(8,128)(2,1)} %get-tuple-element.736, s32[]{:T(128)S(6)} %select_n.1126, s32[]{:T(128)S(6)} %select_n.1127, s32[]{:T(128)S(6)} %select_n.1128, s32[]{:T(128)S(6)} %select_n.1129, s32[]{:T(128)S(6)} %select_n.1130, ...), kind=kLoop, calls=%fused_computation.112.clone.1 | loop fusion | flops 34078720 | bytes 21235776 | tf_op jit(solution)/shard_map/while/body/add | solution.py:70
  322.5 10.1 %fusion.146 = f32[128,4096]{1,0:T(8,128)S(1)} fusion(f32[128,4096]{1,0:T(8,128)S(1)} %copy-done.2, f32[4096]{0:T(1024)S(1)} %bitcast.124, f32[4096]{0:T(1024)S(1)} %bitcast.126, f32[4096]{0:T(1024)S(1)} %bitcast.128, f32[4096]{0:T(1024)S(1)} %bitcast.130, f32[4096]{0:T(1024)S(1)} %bitcast.132, f32[4096]{0:T(1024)S(1)} %bitcast.134, ...), kind=kLoop, calls=%fused_computation.49.clone.1 | loop fusion | flops 34078720 | bytes 21235776 | tf_op jit(solution)/shard_map/while/body/add | solution.py:61
  334.1 6.7 fusion.150
  374.2 15.8 %fusion.148 = f32[128,4096]{1,0:T(8,128)} fusion(f32[128,4096]{1,0:T(8,128)} %get-tuple-element.669, bf16[256,4096]{1,0:T(8,128)(2,1)} %get-tuple-element.736, s32[]{:T(128)S(6)} %select_n.1126, s32[]{:T(128)S(6)} %select_n.1127, s32[]{:T(128)S(6)} %select_n.1128, s32[]{:T(128)S(6)} %select_n.1129, s32[]{:T(128)S(6)} %select_n.1130, ...), kind=kLoop, calls=%fused_computation.112.clone.1 | loop fusion | flops 34078720 | bytes 21235776 | tf_op jit(solution)/shard_map/while/body/add | solution.py:70
  390.0 10.1 %fusion.146 = f32[128,4096]{1,0:T(8,128)S(1)} fusion(f32[128,4096]{1,0:T(8,128)S(1)} %copy-done.2, f32[4096]{0:T(1024)S(1)} %bitcast.124, f32[4096]{0:T(1024)S(1)} %bitcast.126, f32[4096]{0:T(1024)S(1)} %bitcast.128, f32[4096]{0:T(1024)S(1)} %bitcast.130, f32[4096]{0:T(1024)S(1)} %bitcast.132, f32[4096]{0:T(1024)S(1)} %bitcast.134, ...), kind=kLoop, calls=%fused_computation.49.clone.1 | loop fusion | flops 34078720 | bytes 21235776 | tf_op jit(solution)/shard_map/while/body/add | solution.py:61
  401.6 6.7 fusion.150
  441.6 15.6 %fusion.148 = f32[128,4096]{1,0:T(8,128)} fusion(f32[128,4096]{1,0:T(8,128)} %get-tuple-element.669, bf16[256,4096]{1,0:T(8,128)(2,1)} %get-tuple-element.736, s32[]{:T(128)S(6)} %select_n.1126, s32[]{:T(128)S(6)} %select_n.1127, s32[]{:T(128)S(6)} %select_n.1128, s32[]{:T(128)S(6)} %select_n.1129, s32[]{:T(128)S(6)} %select_n.1130, ...), kind=kLoop, calls=%fused_computation.112.clone.1 | loop fusion | flops 34078720 | bytes 21235776 | tf_op jit(solution)/shard_map/while/body/add | solution.py:70
  457.3 10.1 %fusion.146 = f32[128,4096]{1,0:T(8,128)S(1)} fusion(f32[128,4096]{1,0:T(8,128)S(1)} %copy-done.2, f32[4096]{0:T(1024)S(1)} %bitcast.124, f32[4096]{0:T(1024)S(1)} %bitcast.126, f32[4096]{0:T(1024)S(1)} %bitcast.128, f32[4096]{0:T(1024)S(1)} %bitcast.130, f32[4096]{0:T(1024)S(1)} %bitcast.132, f32[4096]{0:T(1024)S(1)} %bitcast.134, ...), kind=kLoop, calls=%fused_computation.49.clone.1 | loop fusion | flops 34078720 | bytes 21235776 | tf_op jit(solution)/shard_map/while/body/add | solution.py:61
  468.9 6.7 fusion.150
  508.9 16.1 %fusion.148 = f32[128,4096]{1,0:T(8,128)} fusion(f32[128,4096]{1,0:T(8,128)} %get-tuple-element.669, bf16[256,4096]{1,0:T(8,128)(2,1)} %get-tuple-element.736, s32[]{:T(128)S(6)} %select_n.1126, s32[]{:T(128)S(6)} %select_n.1127, s32[]{:T(128)S(6)} %select_n.1128, s32[]{:T(128)S(6)} %select_n.1129, s32[]{:T(128)S(6)} %select_n.1130, ...), kind=kLoop, calls=%fused_computation.112.clone.1 | loop fusion | flops 34078720 | bytes 21235776 | tf_op jit(solution)/shard_map/while/body/add | solution.py:70
  525.0 10.1 %fusion.146 = f32[128,4096]{1,0:T(8,128)S(1)} fusion(f32[128,4096]{1,0:T(8,128)S(1)} %copy-done.2, f32[4096]{0:T(1024)S(1)} %bitcast.124, f32[4096]{0:T(1024)S(1)} %bitcast.126, f32[4096]{0:T(1024)S(1)} %bitcast.128, f32[4096]{0:T(1024)S(1)} %bitcast.130, f32[4096]{0:T(1024)S(1)} %bitcast.132, f32[4096]{0:T(1024)S(1)} %bitcast.134, ...), kind=kLoop, calls=%fused_computation.49.clone.1 | loop fusion | flops 34078720 | bytes 21235776 | tf_op jit(solution)/shard_map/while/body/add | solution.py:61
  536.6 6.7 fusion.150
  576.9 16.1 %fusion.148 = f32[128,4096]{1,0:T(8,128)} fusion(f32[128,4096]{1,0:T(8,128)} %get-tuple-element.669, bf16[256,4096]{1,0:T(8,128)(2,1)} %get-tuple-element.736, s32[]{:T(128)S(6)} %select_n.1126, s32[]{:T(128)S(6)} %select_n.1127, s32[]{:T(128)S(6)} %select_n.1128, s32[]{:T(128)S(6)} %select_n.1129, s32[]{:T(128)S(6)} %select_n.1130, ...), kind=kLoop, calls=%fused_computation.112.clone.1 | loop fusion | flops 34078720 | bytes 21235776 | tf_op jit(solution)/shard_map/while/body/add | solution.py:70
  592.9 10.1 %fusion.146 = f32[128,4096]{1,0:T(8,128)S(1)} fusion(f32[128,4096]{1,0:T(8,128)S(1)} %copy-done.2, f32[4096]{0:T(1024)S(1)} %bitcast.124, f32[4096]{0:T(1024)S(1)} %bitcast.126, f32[4096]{0:T(1024)S(1)} %bitcast.128, f32[4096]{0:T(1024)S(1)} %bitcast.130, f32[4096]{0:T(1024)S(1)} %bitcast.132, f32[4096]{0:T(1024)S(1)} %bitcast.134, ...), kind=kLoop, calls=%fused_computation.49.clone.1 | loop fusion | flops 34078720 | bytes 21235776 | tf_op jit(solution)/shard_map/while/body/add | solution.py:61
  612.3 47.3 %reduce-scatter.2.cloned.1.call-done = f32[32,4096]{1,0:T(8,128)} async-done(((f32[128,4096]{1,0:T(8,128)}), f32[32,4096]{1,0:T(8,128)}) %reduce-scatter.2.cloned.1.call-update) | async-done | bytes 524304 | tf_op jit(solution)/shard_map/reduce_scatter | solution.py:87
  662.6 112.8 %all-reduce.2.cloned.1.call-done = f32[32,4096]{1,0:T(8,128)} async-done(((f32[32,4096]{1,0:T(8,128)}), f32[32,4096]{1,0:T(8,128)}) %all-reduce.2.cloned.1.call-update) | async-done | bytes 524304 | tf_op jit(solution)/shard_map/psum | solution.py:86
  (242 shorter events, 300.0 us)
Async XLA Ops:
  7.2 7.9 %copy-start.5 = (bf16[1,128,4096]{2,1,0:T(8,128)(2,1)S(1)}, bf16[1,128,4096]{2,1,0:T(8,128)(2,1)}, u32[]{:S(2)}) copy-start(bf16[1,128,4096]{2,1,0:T(8,128)(2,1)} %param.12) | copy-start | bytes 3145732
  7.2 55.2 %all-gather.2.cloned.1.call-start = ((), (), s32[]{:S(2)}) async-start(), calls=%async_computation.1 | async-start | bytes 2621440 | tf_op jit(solution)/shard_map/all_gather | solution.py:22
  7.9 651.6 %reduce-scatter.2.cloned.1.call-start = ((), (), s32[]{:S(2)}) async-start(), calls=%async_computation.2 | async-start | bytes 2621440 | tf_op jit(solution)/shard_map/reduce_scatter | solution.py:87
  8.0 7.1 copy-start.7
  9.8 6.8 copy-start.6
  9.9 16.2 %collective-permute-start = (bf16[128,4096]{1,0:T(8,128)(2,1)S(1)}, bf16[128,4096]{1,0:T(8,128)(2,1)}, u32[]{:S(2)}, u32[]{:S(2)}) collective-permute-start(bf16[128,4096]{1,0:T(8,128)(2,1)S(1)} %fusion.132), channel_id=1, source_target_pairs={{0,8},{8,16},{16,24},{24,32},{32,40},{40,48},{48,56},{56,64},{64,7... | collective-permute-start | bytes 3145736 | tf_op jit(solution)/shard_map/ppermute | solution.py:13
  16.7 4.0 copy-start.8
  17.7 16.7 %collective-permute-start.1 = (bf16[128,4096]{1,0:T(8,128)(2,1)}, bf16[128,4096]{1,0:T(8,128)(2,1)}, u32[]{:S(2)}, u32[]{:S(2)}) collective-permute-start(bf16[128,4096]{1,0:T(8,128)(2,1)} %broadcast_select_fusion), channel_id=1, source_target_pairs={{8,0},{16,8},{24,16},{32,24},{40,32},{48,40},{56,48},{64,56},{72,6... | collective-permute-start | bytes 3145736 | tf_op jit(solution)/shard_map/ppermute | solution.py:13
  64.1 6.7 copy-start
  104.1 15.4 %copy-start.2 = (f32[128,4096]{1,0:T(8,128)S(1)}, f32[128,4096]{1,0:T(8,128)}, u32[]{:S(2)}) copy-start(f32[128,4096]{1,0:T(8,128)} %get-tuple-element.668) | copy-start | bytes 6291460 | tf_op jit(solution)/shard_map/while
  129.7 1.3 copy-start.3
  131.2 6.7 copy-start
  171.3 15.7 %copy-start.2 = (f32[128,4096]{1,0:T(8,128)S(1)}, f32[128,4096]{1,0:T(8,128)}, u32[]{:S(2)}) copy-start(f32[128,4096]{1,0:T(8,128)} %get-tuple-element.668) | copy-start | bytes 6291460 | tf_op jit(solution)/shard_map/while
  197.2 1.3 copy-start.3
  198.7 6.7 copy-start
  238.9 15.9 %copy-start.2 = (f32[128,4096]{1,0:T(8,128)S(1)}, f32[128,4096]{1,0:T(8,128)}, u32[]{:S(2)}) copy-start(f32[128,4096]{1,0:T(8,128)} %get-tuple-element.668) | copy-start | bytes 6291460 | tf_op jit(solution)/shard_map/while
  265.0 1.3 copy-start.3
  266.5 6.7 copy-start
  306.4 16.1 %copy-start.2 = (f32[128,4096]{1,0:T(8,128)S(1)}, f32[128,4096]{1,0:T(8,128)}, u32[]{:S(2)}) copy-start(f32[128,4096]{1,0:T(8,128)} %get-tuple-element.668) | copy-start | bytes 6291460 | tf_op jit(solution)/shard_map/while
  334.1 6.7 copy-start
  374.2 15.8 %copy-start.2 = (f32[128,4096]{1,0:T(8,128)S(1)}, f32[128,4096]{1,0:T(8,128)}, u32[]{:S(2)}) copy-start(f32[128,4096]{1,0:T(8,128)} %get-tuple-element.668) | copy-start | bytes 6291460 | tf_op jit(solution)/shard_map/while
  400.1 1.3 copy-start.3
  401.6 6.7 copy-start
  441.6 15.6 %copy-start.2 = (f32[128,4096]{1,0:T(8,128)S(1)}, f32[128,4096]{1,0:T(8,128)}, u32[]{:S(2)}) copy-start(f32[128,4096]{1,0:T(8,128)} %get-tuple-element.668) | copy-start | bytes 6291460 | tf_op jit(solution)/shard_map/while
  467.4 1.3 copy-start.3
  468.9 6.7 copy-start
  508.9 16.1 %copy-start.2 = (f32[128,4096]{1,0:T(8,128)S(1)}, f32[128,4096]{1,0:T(8,128)}, u32[]{:S(2)}) copy-start(f32[128,4096]{1,0:T(8,128)} %get-tuple-element.668) | copy-start | bytes 6291460 | tf_op jit(solution)/shard_map/while
  536.6 6.7 copy-start
  576.9 16.1 %copy-start.2 = (f32[128,4096]{1,0:T(8,128)S(1)}, f32[128,4096]{1,0:T(8,128)}, u32[]{:S(2)}) copy-start(f32[128,4096]{1,0:T(8,128)} %get-tuple-element.668) | copy-start | bytes 6291460 | tf_op jit(solution)/shard_map/while
  604.4 3.3 copy-start.4
  607.6 1.6 copy-start.1
  607.6 167.7 %all-reduce.2.cloned.1.call-start = ((), (), s32[]{:S(2)}) async-start(), calls=%async_computation.3 | async-start | bytes 1048576 | tf_op jit(solution)/shard_map/psum | solution.py:86
  (3 other events, 4.0 us)
Sparse Core Ops, SparseCore 0:
  9.8 52.5 all-gather.1
  607.7 51.7 reduce-scatter.1
  663.0 112.2 all-reduce.1
where the time goes:
time: 787 us; the launch traced here: 784 us
  other arithmetic  323 us (41%)
  local copies, waits for them, and re-layouts  240 us (30%)
  waiting for transfers between devices  198 us (25%)
  between operations  14.5 us (2%)
    dynamic_update_slice x128, local copies, waits for them, and re-layouts, tap_block(): lax.dynamic_update_slice_in_dim(filt_grad, tap_term[None, :], tap_index, 0)  205 us
    add x8, other arithmetic, tap_block(): grad_back = grad_back + jnp.where(reaching, ahead_rows * weight_row, 0.0)  127 us
    psum x1, waiting for transfers between devices, shards(): summed_all = lax.psum(filt_grad, 'ctx')  113 us
    reduce_sum x16, other arithmetic, tap_block(): tap_term = jnp.sum(jnp.where(inside, grad_wide * earlier, 0.0), axis=0)  95.8 us
    add x8, other arithmetic, tap_block(): conv_out = conv_out + jnp.where(inside, earlier * weight_row, 0.0)  80.8 us
    reduce_scatter x1, waiting for transfers between devices, shards(): lax.psum_scatter(summed_all, 'fsdp', scatter_dimension=0, tiled=True)  47.3 us
    all_gather x1, waiting for transfers between devices, shards(): weights = lax.all_gather(filters, 'fsdp', axis=0, tiled=True)  25.2 us
    dynamic_slice x8, local copies, waits for them, and re-layouts, tap_block(): weight_row = lax.dynamic_slice_in_dim(weights, tap_index, 1, 0)  19.3 us
  transfers between devices with their start and end apart: 5, of which 5 were waited for; matrix products, arithmetic and copies ran while one was open for 2% of the time, Pallas kernels for 0%

commit v1 on v0

--- a/solution.py
+++ b/solution.py
@@ -83,7 +83,13 @@
     grad_value = (grad_back * key_local.astype(jnp.float32)).astype(jnp.bfloat16)
     norm_scale = 1.0 / math.sqrt(lax.axis_size("fsdp") * lax.axis_size("ctx") * length)
     filt_grad = filt_grad * norm_scale
-    summed_all = lax.psum(filt_grad, "ctx")
+    size = lax.axis_size("ctx")
+    summed_all, reach = (filt_grad, 1)
+    while reach < size:
+        summed_all = summed_all + lax.ppermute(
+            summed_all, "ctx", [(i_2, i_2 ^ reach) for i_2 in range(size)]
+        )
+        reach = 2 * reach
     share_out = lax.psum_scatter(summed_all, "fsdp", scatter_dimension=0, tiled=True)
     return (grad_query[None], grad_key[None], grad_value[None], share_out)
 

time: 787 us -> 864 us (1.098)
  waiting for transfers between devices: 198 us -> 266 us
  starting transfers between devices: 7.53 us -> 18.1 us
    ppermute x0 -> x5, waiting for transfers between devices: none -> 183 us  [shards(): lax.ppermute(summed_all, 'ctx', [(i_2, i_2 ^ reach) for i_2 in range(size)])]
    psum x1 -> x0, waiting for transfers between devices: 113 us -> none  [shards(): summed_all = lax.psum(filt_grad, 'ctx')]
    ppermute x0 -> x5, starting transfers between devices: none -> 10.6 us  [shards(): lax.ppermute(summed_all, 'ctx', [(i_2, i_2 ^ reach) for i_2 in range(size)])]
  transfers between devices with their start and end apart: 5 -> 9, of which waited for: 5 -> 9; matrix products, arithmetic and copies ran while one was open for 2% -> 2% of each run, Pallas kernels for 0% -> 0%
where the time goes in v1:
time: 864 us; the launch traced here: 861 us
  other arithmetic  323 us (37%)
  waiting for transfers between devices  266 us (31%)
  local copies, waits for them, and re-layouts  238 us (28%)
  starting transfers between devices  18.1 us (2%)
  between operations  14.9 us (2%)
    dynamic_update_slice x128, local copies, waits for them, and re-layouts, tap_block(): lax.dynamic_update_slice_in_dim(filt_grad, tap_term[None, :], tap_index, 0)  205 us
    ppermute x5, waiting for transfers between devices, shards(): lax.ppermute(summed_all, 'ctx', [(i_2, i_2 ^ reach) for i_2 in range(size)])  183 us
    add x8, other arithmetic, tap_block(): grad_back = grad_back + jnp.where(reaching, ahead_rows * weight_row, 0.0)  127 us
    reduce_sum x16, other arithmetic, tap_block(): tap_term = jnp.sum(jnp.where(inside, grad_wide * earlier, 0.0), axis=0)  95.8 us
    add x8, other arithmetic, tap_block(): conv_out = conv_out + jnp.where(inside, earlier * weight_row, 0.0)  80.8 us
    reduce_scatter x1, waiting for transfers between devices, shards(): lax.psum_scatter(summed_all, 'fsdp', scatter_dimension=0, tiled=True)  45.1 us
    all_gather x1, waiting for transfers between devices, shards(): weights = lax.all_gather(filters, 'fsdp', axis=0, tiled=True)  25.2 us
    dynamic_slice x8, local copies, waits for them, and re-layouts, tap_block(): weight_row = lax.dynamic_slice_in_dim(weights, tap_index, 1, 0)  19.3 us
  transfers between devices with their start and end apart: 9, of which 9 were waited for; matrix products, arithmetic and copies ran while one was open for 2% of the time, Pallas kernels for 0%

profile of v1, /device:TPU:1, one launch (start us, length us, event | category | flops | bytes accessed | tf_op | source)
XLA Modules:
  0.0 860.7 jit_solution(12973702303083749387)
XLA Ops:
  28.0 6.5 collective-permute-done.1
  37.2 25.2 %all-gather.2.cloned.1.call-done = f32[128,4096]{1,0:T(8,128)} async-done(((f32[32,4096]{1,0:T(8,128)}), f32[128,4096]{1,0:T(8,128)}) %all-gather.2.cloned.1.call-update) | async-done | bytes 2097168 | tf_op jit(solution)/shard_map/all_gather | solution.py:22
  63.9 540.4 %while.18 = (s32[]{:T(128)}, f32[128,4096]{1,0:T(8,128)}, f32[128,4096]{1,0:T(8,128)}, f32[128,4096]{1,0:T(8,128)}, s32[128]{0:T(128)S(1)}, /*index=5*/bf16[256,...) while((s32[]{:T(128)}, f32[128,4096]{1,0:T(8,128)}, ...), condition=%wide.region_19.20_spmd.clone, body=%wide.region_2.19_spmd.clone.sunk | while | flops 101652864 | bytes 89937200 | solution.py:78
  64.1 6.7 fusion.151
  104.1 15.4 %fusion.149 = f32[128,4096]{1,0:T(8,128)} fusion(f32[128,4096]{1,0:T(8,128)} %get-tuple-element.669, bf16[256,4096]{1,0:T(8,128)(2,1)} %get-tuple-element.736, s32[]{:T(128)S(6)} %select_n.1126, s32[]{:T(128)S(6)} %select_n.1127, s32[]{:T(128)S(6)} %select_n.1128, s32[]{:T(128)S(6)} %select_n.1129, s32[]{:T(128)S(6)} %select_n.1130, ...), kind=kLoop, calls=%fused_computation.112.clone.1 | loop fusion | flops 34078720 | bytes 21235776 | tf_op jit(solution)/shard_map/while/body/add | solution.py:70
  119.5 10.1 %fusion.147 = f32[128,4096]{1,0:T(8,128)S(1)} fusion(f32[128,4096]{1,0:T(8,128)S(1)} %copy-done.2, f32[4096]{0:T(1024)S(1)} %bitcast.124, f32[4096]{0:T(1024)S(1)} %bitcast.126, f32[4096]{0:T(1024)S(1)} %bitcast.128, f32[4096]{0:T(1024)S(1)} %bitcast.130, f32[4096]{0:T(1024)S(1)} %bitcast.132, f32[4096]{0:T(1024)S(1)} %bitcast.134, ...), kind=kLoop, calls=%fused_computation.49.clone.1 | loop fusion | flops 34078720 | bytes 21235776 | tf_op jit(solution)/shard_map/while/body/add | solution.py:61
  131.2 6.7 fusion.151
  171.3 15.7 %fusion.149 = f32[128,4096]{1,0:T(8,128)} fusion(f32[128,4096]{1,0:T(8,128)} %get-tuple-element.669, bf16[256,4096]{1,0:T(8,128)(2,1)} %get-tuple-element.736, s32[]{:T(128)S(6)} %select_n.1126, s32[]{:T(128)S(6)} %select_n.1127, s32[]{:T(128)S(6)} %select_n.1128, s32[]{:T(128)S(6)} %select_n.1129, s32[]{:T(128)S(6)} %select_n.1130, ...), kind=kLoop, calls=%fused_computation.112.clone.1 | loop fusion | flops 34078720 | bytes 21235776 | tf_op jit(solution)/shard_map/while/body/add | solution.py:70
  187.1 10.1 %fusion.147 = f32[128,4096]{1,0:T(8,128)S(1)} fusion(f32[128,4096]{1,0:T(8,128)S(1)} %copy-done.2, f32[4096]{0:T(1024)S(1)} %bitcast.124, f32[4096]{0:T(1024)S(1)} %bitcast.126, f32[4096]{0:T(1024)S(1)} %bitcast.128, f32[4096]{0:T(1024)S(1)} %bitcast.130, f32[4096]{0:T(1024)S(1)} %bitcast.132, f32[4096]{0:T(1024)S(1)} %bitcast.134, ...), kind=kLoop, calls=%fused_computation.49.clone.1 | loop fusion | flops 34078720 | bytes 21235776 | tf_op jit(solution)/shard_map/while/body/add | solution.py:61
  198.7 6.7 fusion.151
  238.9 15.9 %fusion.149 = f32[128,4096]{1,0:T(8,128)} fusion(f32[128,4096]{1,0:T(8,128)} %get-tuple-element.669, bf16[256,4096]{1,0:T(8,128)(2,1)} %get-tuple-element.736, s32[]{:T(128)S(6)} %select_n.1126, s32[]{:T(128)S(6)} %select_n.1127, s32[]{:T(128)S(6)} %select_n.1128, s32[]{:T(128)S(6)} %select_n.1129, s32[]{:T(128)S(6)} %select_n.1130, ...), kind=kLoop, calls=%fused_computation.112.clone.1 | loop fusion | flops 34078720 | bytes 21235776 | tf_op jit(solution)/shard_map/while/body/add | solution.py:70
  254.9 10.1 %fusion.147 = f32[128,4096]{1,0:T(8,128)S(1)} fusion(f32[128,4096]{1,0:T(8,128)S(1)} %copy-done.2, f32[4096]{0:T(1024)S(1)} %bitcast.124, f32[4096]{0:T(1024)S(1)} %bitcast.126, f32[4096]{0:T(1024)S(1)} %bitcast.128, f32[4096]{0:T(1024)S(1)} %bitcast.130, f32[4096]{0:T(1024)S(1)} %bitcast.132, f32[4096]{0:T(1024)S(1)} %bitcast.134, ...), kind=kLoop, calls=%fused_computation.49.clone.1 | loop fusion | flops 34078720 | bytes 21235776 | tf_op jit(solution)/shard_map/while/body/add | solution.py:61
  266.5 6.7 fusion.151
  306.4 16.0 %fusion.149 = f32[128,4096]{1,0:T(8,128)} fusion(f32[128,4096]{1,0:T(8,128)} %get-tuple-element.669, bf16[256,4096]{1,0:T(8,128)(2,1)} %get-tuple-element.736, s32[]{:T(128)S(6)} %select_n.1126, s32[]{:T(128)S(6)} %select_n.1127, s32[]{:T(128)S(6)} %select_n.1128, s32[]{:T(128)S(6)} %select_n.1129, s32[]{:T(128)S(6)} %select_n.1130, ...), kind=kLoop, calls=%fused_computation.112.clone.1 | loop fusion | flops 34078720 | bytes 21235776 | tf_op jit(solution)/shard_map/while/body/add | solution.py:70
  322.5 10.1 %fusion.147 = f32[128,4096]{1,0:T(8,128)S(1)} fusion(f32[128,4096]{1,0:T(8,128)S(1)} %copy-done.2, f32[4096]{0:T(1024)S(1)} %bitcast.124, f32[4096]{0:T(1024)S(1)} %bitcast.126, f32[4096]{0:T(1024)S(1)} %bitcast.128, f32[4096]{0:T(1024)S(1)} %bitcast.130, f32[4096]{0:T(1024)S(1)} %bitcast.132, f32[4096]{0:T(1024)S(1)} %bitcast.134, ...), kind=kLoop, calls=%fused_computation.49.clone.1 | loop fusion | flops 34078720 | bytes 21235776 | tf_op jit(solution)/shard_map/while/body/add | solution.py:61
  334.1 6.7 fusion.151
  374.2 15.8 %fusion.149 = f32[128,4096]{1,0:T(8,128)} fusion(f32[128,4096]{1,0:T(8,128)} %get-tuple-element.669, bf16[256,4096]{1,0:T(8,128)(2,1)} %get-tuple-element.736, s32[]{:T(128)S(6)} %select_n.1126, s32[]{:T(128)S(6)} %select_n.1127, s32[]{:T(128)S(6)} %select_n.1128, s32[]{:T(128)S(6)} %select_n.1129, s32[]{:T(128)S(6)} %select_n.1130, ...), kind=kLoop, calls=%fused_computation.112.clone.1 | loop fusion | flops 34078720 | bytes 21235776 | tf_op jit(solution)/shard_map/while/body/add | solution.py:70
  390.0 10.1 %fusion.147 = f32[128,4096]{1,0:T(8,128)S(1)} fusion(f32[128,4096]{1,0:T(8,128)S(1)} %copy-done.2, f32[4096]{0:T(1024)S(1)} %bitcast.124, f32[4096]{0:T(1024)S(1)} %bitcast.126, f32[4096]{0:T(1024)S(1)} %bitcast.128, f32[4096]{0:T(1024)S(1)} %bitcast.130, f32[4096]{0:T(1024)S(1)} %bitcast.132, f32[4096]{0:T(1024)S(1)} %bitcast.134, ...), kind=kLoop, calls=%fused_computation.49.clone.1 | loop fusion | flops 34078720 | bytes 21235776 | tf_op jit(solution)/shard_map/while/body/add | solution.py:61
  401.6 6.7 fusion.151
  441.6 15.6 %fusion.149 = f32[128,4096]{1,0:T(8,128)} fusion(f32[128,4096]{1,0:T(8,128)} %get-tuple-element.669, bf16[256,4096]{1,0:T(8,128)(2,1)} %get-tuple-element.736, s32[]{:T(128)S(6)} %select_n.1126, s32[]{:T(128)S(6)} %select_n.1127, s32[]{:T(128)S(6)} %select_n.1128, s32[]{:T(128)S(6)} %select_n.1129, s32[]{:T(128)S(6)} %select_n.1130, ...), kind=kLoop, calls=%fused_computation.112.clone.1 | loop fusion | flops 34078720 | bytes 21235776 | tf_op jit(solution)/shard_map/while/body/add | solution.py:70
  457.3 10.1 %fusion.147 = f32[128,4096]{1,0:T(8,128)S(1)} fusion(f32[128,4096]{1,0:T(8,128)S(1)} %copy-done.2, f32[4096]{0:T(1024)S(1)} %bitcast.124, f32[4096]{0:T(1024)S(1)} %bitcast.126, f32[4096]{0:T(1024)S(1)} %bitcast.128, f32[4096]{0:T(1024)S(1)} %bitcast.130, f32[4096]{0:T(1024)S(1)} %bitcast.132, f32[4096]{0:T(1024)S(1)} %bitcast.134, ...), kind=kLoop, calls=%fused_computation.49.clone.1 | loop fusion | flops 34078720 | bytes 21235776 | tf_op jit(solution)/shard_map/while/body/add | solution.py:61
  468.9 6.7 fusion.151
  508.9 16.1 %fusion.149 = f32[128,4096]{1,0:T(8,128)} fusion(f32[128,4096]{1,0:T(8,128)} %get-tuple-element.669, bf16[256,4096]{1,0:T(8,128)(2,1)} %get-tuple-element.736, s32[]{:T(128)S(6)} %select_n.1126, s32[]{:T(128)S(6)} %select_n.1127, s32[]{:T(128)S(6)} %select_n.1128, s32[]{:T(128)S(6)} %select_n.1129, s32[]{:T(128)S(6)} %select_n.1130, ...), kind=kLoop, calls=%fused_computation.112.clone.1 | loop fusion | flops 34078720 | bytes 21235776 | tf_op jit(solution)/shard_map/while/body/add | solution.py:70
  525.0 10.1 %fusion.147 = f32[128,4096]{1,0:T(8,128)S(1)} fusion(f32[128,4096]{1,0:T(8,128)S(1)} %copy-done.2, f32[4096]{0:T(1024)S(1)} %bitcast.124, f32[4096]{0:T(1024)S(1)} %bitcast.126, f32[4096]{0:T(1024)S(1)} %bitcast.128, f32[4096]{0:T(1024)S(1)} %bitcast.130, f32[4096]{0:T(1024)S(1)} %bitcast.132, f32[4096]{0:T(1024)S(1)} %bitcast.134, ...), kind=kLoop, calls=%fused_computation.49.clone.1 | loop fusion | flops 34078720 | bytes 21235776 | tf_op jit(solution)/shard_map/while/body/add | solution.py:61
  536.6 6.7 fusion.151
  576.9 16.1 %fusion.149 = f32[128,4096]{1,0:T(8,128)} fusion(f32[128,4096]{1,0:T(8,128)} %get-tuple-element.669, bf16[256,4096]{1,0:T(8,128)(2,1)} %get-tuple-element.736, s32[]{:T(128)S(6)} %select_n.1126, s32[]{:T(128)S(6)} %select_n.1127, s32[]{:T(128)S(6)} %select_n.1128, s32[]{:T(128)S(6)} %select_n.1129, s32[]{:T(128)S(6)} %select_n.1130, ...), kind=kLoop, calls=%fused_computation.112.clone.1 | loop fusion | flops 34078720 | bytes 21235776 | tf_op jit(solution)/shard_map/while/body/add | solution.py:70
  592.9 10.1 %fusion.147 = f32[128,4096]{1,0:T(8,128)S(1)} fusion(f32[128,4096]{1,0:T(8,128)S(1)} %copy-done.2, f32[4096]{0:T(1024)S(1)} %bitcast.124, f32[4096]{0:T(1024)S(1)} %bitcast.126, f32[4096]{0:T(1024)S(1)} %bitcast.128, f32[4096]{0:T(1024)S(1)} %bitcast.130, f32[4096]{0:T(1024)S(1)} %bitcast.132, f32[4096]{0:T(1024)S(1)} %bitcast.134, ...), kind=kLoop, calls=%fused_computation.49.clone.1 | loop fusion | flops 34078720 | bytes 21235776 | tf_op jit(solution)/shard_map/while/body/add | solution.py:61
  615.5 45.7 %collective-permute-done.3 = f32[128,4096]{1,0:T(8,128)S(1)} collective-permute-done((f32[128,4096]{1,0:T(8,128)S(1)}, f32[128,4096]{1,0:T(8,128)S(1)}, u32[]{:S(2)}, u32[]{:S(2)}) %collective-permute-start.3) | collective-permute-done | bytes 2097184 | tf_op jit(solution)/shard_map/ppermute | solution.py:89
  664.0 45.2 %collective-permute-done.4 = f32[128,4096]{1,0:T(8,128)S(1)} collective-permute-done((f32[128,4096]{1,0:T(8,128)S(1)}, f32[128,4096]{1,0:T(8,128)S(1)}, u32[]{:S(2)}, u32[]{:S(2)}) %collective-permute-start.4) | collective-permute-done | bytes 2097184 | tf_op jit(solution)/shard_map/ppermute | solution.py:89
  710.3 44.6 %collective-permute-done.5 = f32[128,4096]{1,0:T(8,128)S(1)} collective-permute-done((f32[128,4096]{1,0:T(8,128)S(1)}, f32[128,4096]{1,0:T(8,128)S(1)}, u32[]{:S(2)}, u32[]{:S(2)}) %collective-permute-start.5) | collective-permute-done | bytes 2097184 | tf_op jit(solution)/shard_map/ppermute | solution.py:89
  757.2 44.0 %collective-permute-done.6 = f32[128,4096]{1,0:T(8,128)S(1)} collective-permute-done((f32[128,4096]{1,0:T(8,128)S(1)}, f32[128,4096]{1,0:T(8,128)S(1)}, u32[]{:S(2)}, u32[]{:S(2)}) %collective-permute-start.6) | collective-permute-done | bytes 2097184 | tf_op jit(solution)/shard_map/ppermute | solution.py:89
  808.8 45.1 %reduce-scatter.2.cloned.1.call-done = f32[32,4096]{1,0:T(8,128)} async-done(((f32[128,4096]{1,0:T(8,128)}), f32[32,4096]{1,0:T(8,128)}) %reduce-scatter.2.cloned.1.call-update) | async-done | bytes 524304 | tf_op jit(solution)/shard_map/reduce_scatter | solution.py:93
  (259 shorter events, 328.1 us)
Async XLA Ops:
  7.2 7.9 copy-start.5
  7.2 55.2 %all-gather.2.cloned.1.call-start = ((), (), s32[]{:S(2)}) async-start(), calls=%async_computation.1 | async-start | bytes 2621440 | tf_op jit(solution)/shard_map/all_gather | solution.py:22
  7.9 846.0 %reduce-scatter.2.cloned.1.call-start = ((), (), s32[]{:S(2)}) async-start(), calls=%async_computation.2 | async-start | bytes 2621440 | tf_op jit(solution)/shard_map/reduce_scatter | solution.py:93
  8.0 7.1 copy-start.10
  9.8 6.8 copy-start.9
  9.9 16.2 %collective-permute-start = (bf16[128,4096]{1,0:T(8,128)(2,1)S(1)}, bf16[128,4096]{1,0:T(8,128)(2,1)}, u32[]{:S(2)}, u32[]{:S(2)}) collective-permute-start(bf16[128,4096]{1,0:T(8,128)(2,1)S(1)} %fusion.132), channel_id=1, source_target_pairs={{0,8},{8,16},{16,24},{24,32},{32,40},{40,48},{48,56},{56,64},{64,7... | collective-permute-start | bytes 3145736 | tf_op jit(solution)/shard_map/ppermute | solution.py:13
  16.7 4.0 copy-start.11
  17.7 16.7 %collective-permute-start.1 = (bf16[128,4096]{1,0:T(8,128)(2,1)}, bf16[128,4096]{1,0:T(8,128)(2,1)}, u32[]{:S(2)}, u32[]{:S(2)}) collective-permute-start(bf16[128,4096]{1,0:T(8,128)(2,1)} %broadcast_select_fusion), channel_id=1, source_target_pairs={{8,0},{16,8},{24,16},{32,24},{40,32},{48,40},{56,48},{64,56},{72,6... | collective-permute-start | bytes 3145736 | tf_op jit(solution)/shard_map/ppermute | solution.py:13
  64.1 6.7 copy-start
  104.1 15.4 %copy-start.2 = (f32[128,4096]{1,0:T(8,128)S(1)}, f32[128,4096]{1,0:T(8,128)}, u32[]{:S(2)}) copy-start(f32[128,4096]{1,0:T(8,128)} %get-tuple-element.668) | copy-start | bytes 6291460 | tf_op jit(solution)/shard_map/while
  131.2 6.7 copy-start
  171.3 15.7 %copy-start.2 = (f32[128,4096]{1,0:T(8,128)S(1)}, f32[128,4096]{1,0:T(8,128)}, u32[]{:S(2)}) copy-start(f32[128,4096]{1,0:T(8,128)} %get-tuple-element.668) | copy-start | bytes 6291460 | tf_op jit(solution)/shard_map/while
  198.7 6.7 copy-start
  238.9 15.9 %copy-start.2 = (f32[128,4096]{1,0:T(8,128)S(1)}, f32[128,4096]{1,0:T(8,128)}, u32[]{:S(2)}) copy-start(f32[128,4096]{1,0:T(8,128)} %get-tuple-element.668) | copy-start | bytes 6291460 | tf_op jit(solution)/shard_map/while
  266.5 6.7 copy-start
  306.4 16.1 %copy-start.2 = (f32[128,4096]{1,0:T(8,128)S(1)}, f32[128,4096]{1,0:T(8,128)}, u32[]{:S(2)}) copy-start(f32[128,4096]{1,0:T(8,128)} %get-tuple-element.668) | copy-start | bytes 6291460 | tf_op jit(solution)/shard_map/while
  334.1 6.7 copy-start
  374.2 15.8 %copy-start.2 = (f32[128,4096]{1,0:T(8,128)S(1)}, f32[128,4096]{1,0:T(8,128)}, u32[]{:S(2)}) copy-start(f32[128,4096]{1,0:T(8,128)} %get-tuple-element.668) | copy-start | bytes 6291460 | tf_op jit(solution)/shard_map/while
  401.6 6.7 copy-start
  441.6 15.6 %copy-start.2 = (f32[128,4096]{1,0:T(8,128)S(1)}, f32[128,4096]{1,0:T(8,128)}, u32[]{:S(2)}) copy-start(f32[128,4096]{1,0:T(8,128)} %get-tuple-element.668) | copy-start | bytes 6291460 | tf_op jit(solution)/shard_map/while
  468.9 6.7 copy-start
  508.9 16.1 %copy-start.2 = (f32[128,4096]{1,0:T(8,128)S(1)}, f32[128,4096]{1,0:T(8,128)}, u32[]{:S(2)}) copy-start(f32[128,4096]{1,0:T(8,128)} %get-tuple-element.668) | copy-start | bytes 6291460 | tf_op jit(solution)/shard_map/while
  536.6 6.7 copy-start
  576.9 16.1 %copy-start.2 = (f32[128,4096]{1,0:T(8,128)S(1)}, f32[128,4096]{1,0:T(8,128)}, u32[]{:S(2)}) copy-start(f32[128,4096]{1,0:T(8,128)} %get-tuple-element.668) | copy-start | bytes 6291460 | tf_op jit(solution)/shard_map/while
  604.4 6.5 copy-start.4
  606.3 4.6 collective-permute-start.2
  611.2 50.0 %collective-permute-start.3 = (f32[128,4096]{1,0:T(8,128)S(1)}, f32[128,4096]{1,0:T(8,128)S(1)}, u32[]{:S(2)}, u32[]{:S(2)}) collective-permute-start(f32[128,4096]{1,0:T(8,128)S(1)} %fusion.137), channel_id=1, source_target_pairs={{0,16},{8,24},{16,0},{24,8},{32,48},{40,56},{48,32},{56,40},{64,80... | collective-permute-start | bytes 6291464 | tf_op jit(solution)/shard_map/ppermute | solution.py:89
  661.4 47.9 %collective-permute-start.4 = (f32[128,4096]{1,0:T(8,128)S(1)}, f32[128,4096]{1,0:T(8,128)S(1)}, u32[]{:S(2)}, u32[]{:S(2)}) collective-permute-start(f32[128,4096]{1,0:T(8,128)S(1)} %add.854), channel_id=1, source_target_pairs={{0,32},{8,40},{16,48},{24,56},{32,0},{40,8},{48,16},{56,24},{64,96... | collective-permute-start | bytes 6291464 | tf_op jit(solution)/shard_map/ppermute | solution.py:89
  709.5 45.4 %collective-permute-start.5 = (f32[128,4096]{1,0:T(8,128)S(1)}, f32[128,4096]{1,0:T(8,128)S(1)}, u32[]{:S(2)}, u32[]{:S(2)}) collective-permute-start(f32[128,4096]{1,0:T(8,128)S(1)} %add.855), channel_id=1, source_target_pairs={{0,64},{8,72},{16,80},{24,88},{32,96},{40,104},{48,112},{56,120},{... | collective-permute-start | bytes 6291464 | tf_op jit(solution)/shard_map/ppermute | solution.py:89
  755.2 46.0 %collective-permute-start.6 = (f32[128,4096]{1,0:T(8,128)S(1)}, f32[128,4096]{1,0:T(8,128)S(1)}, u32[]{:S(2)}, u32[]{:S(2)}) collective-permute-start(f32[128,4096]{1,0:T(8,128)S(1)} %add.856), channel_id=1, source_target_pairs={{0,128},{8,136},{16,144},{24,152},{32,160},{40,168},{48,176},{56,1... | collective-permute-start | bytes 6291464 | tf_op jit(solution)/shard_map/ppermute | solution.py:89
  804.0 2.9 copy-start.7
  804.0 2.9 copy-start.8
  (10 other events, 14.9 us)
Sparse Core Ops, SparseCore 0:
  9.8 52.5 all-gather.1
  803.0 50.8 reduce-scatter.1
